TPU v7x, 32 devices: a whole 2x2x4 slice. The times are simulated.
32 devices in a mesh: seq: 16 (over z, y, x), head: 2 (over core).
Axes of the slice: x: 2, y: 2, z: 4, core: 2. Of those that a mesh axis runs over, the one named last changes fastest.
Arguments:
- queries: bfloat16 [4096, 2048], P('seq', 'head'), may hold values from -12 to 12
- key_vectors: bfloat16 [4096, 2048], P('seq', 'head'), may hold values from -12 to 12
- value_vectors: bfloat16 [4096, 2048], P('seq', 'head'), may hold values from -32 to 32
- gain_query: float32 [128], replicated, may hold values from 0.1 to 1.9
- gain_key: float32 [128], replicated, may hold values from 0.1 to 1.9
- grad_out: bfloat16 [4096, 2048], P('seq', 'head'), may hold values from -24 to 24
Outputs:
- attended: bfloat16 [4096, 2048], P('seq', 'head')
- grad_query: bfloat16 [4096, 2048], P('seq', 'head')
- grad_key: bfloat16 [4096, 2048], P('seq', 'head')
- grad_value: bfloat16 [4096, 2048], P('seq', 'head')
- gain_grads: float32 [2, 128], replicated
All inputs are finite; a program needn't handle non-finite values.
Results may differ from a plain program's by a relative error of at most 0.039.
Values may be sent and summed in bfloat16 or wider, within the bound.
A program may use at most 128 MiB of HBM per device.

v0:
```python
import functools
import math

import jax
import jax.numpy as jnp
from jax import lax
from jax.experimental import pallas as pl
from jax.experimental.pallas import tpu as pltpu
from jax.sharding import PartitionSpec as P

HEADS = 16
DH = 128
QUAD = 4
EPS = 1e-06
F32 = jnp.float32
BF16 = jnp.bfloat16


def flip(index, mask):
    result = index
    bit = 0
    while mask >> bit:
        if (mask >> bit) & 1:
            own = lax.rem(lax.div(index, 1 << bit), 2)
            result = result + (1 - 2 * own) * (1 << bit)
        bit += 1
    return result


def dot_nn(a, b):
    return lax.dot_general(a, b, (((1,), (0,)), ((), ())), preferred_element_type=F32)


def dot_nt(a, b):
    return lax.dot_general(a, b, (((1,), (1,)), ((), ())), preferred_element_type=F32)


def dot_tn(a, b):
    return lax.dot_general(a, b, (((0,), (0,)), ((), ())), preferred_element_type=F32)


def tiled(lanes, width):
    return jnp.concatenate([lanes] * (width // lanes.shape[1]), axis=1)


def kernel(
    seq_count, rows, own_heads,
    q_hbm, k_hbm, v_hbm, g_hbm, gain_q, gain_k,
    att_hbm, dq_hbm, dk_hbm, dv_hbm, gain_out,
    rin, oout, qp, kvp, rkv, gsend, grecv, wide, num, den, gnp, gdp, gqp, gkp, gvp,
    pair_p, one_p, up_p, gains, gacc, ga, gb, gc,
    in_s, in_r, out_s, out_r, kv_s, kv_r, gr_s, gr_r, ga_s, ga_r, gb_s, gb_r, gc_s, gc_r, gain_s,
):
    depth = seq_count.bit_length() - 1
    groups = seq_count // QUAD
    total = QUAD * rows
    inv_root = 1.0 / math.sqrt(DH)
    exp_scale = inv_root * math.log2(math.e)
    level_rows = [total >> j for j in range(depth)]
    offs = [2 * total - 2 * (total >> j) for j in range(depth)]
    me = lax.axis_index("seq")
    core = lax.axis_index("head")
    member = lax.rem(me, QUAD)
    inputs = (q_hbm, k_hbm, v_hbm, g_hbm)
    outputs = (att_hbm, dq_hbm, dk_hbm, dv_hbm)

    def col(index, h):
        return pl.ds(pl.multiple_of((index * own_heads + h) * DH, DH), DH)

    def rowset(index):
        return pl.ds(pl.multiple_of(index * rows, rows), rows)

    def in_copy(a, h, x):
        if x == 0:
            return pltpu.make_async_copy(
                inputs[a].at[:, col(member, h)], rin.at[a, h, rowset(member)], in_r.at[a, h, 0]
            )
        return pltpu.make_async_remote_copy(
            inputs[a].at[:, col(flip(member, x), h)],
            rin.at[a, h, rowset(member)],
            in_s.at[a, h, x],
            in_r.at[a, h, x],
            device_id={"seq": flip(me, x)},
            device_id_type=pl.DeviceIdType.MESH,
        )

    def out_copy(a, h, x):
        if x == 0:
            return pltpu.make_async_copy(
                oout.at[a, h, rowset(member)], outputs[a].at[:, col(member, h)], out_r.at[a, h, 0]
            )
        return pltpu.make_async_remote_copy(
            oout.at[a, h, rowset(flip(member, x))],
            outputs[a].at[:, col(member, h)],
            out_s.at[a, h, x],
            out_r.at[a, h, x],
            device_id={"seq": flip(me, x)},
            device_id_type=pl.DeviceIdType.MESH,
        )

    def peer_level(d):
        j = 1 + d.bit_length()
        return j, d - (1 << (j - 2))

    def kv_copy(h, d):
        j, t = peer_level(d)
        n = level_rows[j]
        return pltpu.make_async_remote_copy(
            kvp.at[h, :, pl.ds(offs[j], n)],
            rkv.at[h, j - 2, :, pl.ds(t * n, n)],
            kv_s.at[h, d],
            kv_r.at[h, d],
            device_id={"seq": flip(me, QUAD * d)},
            device_id_type=pl.DeviceIdType.MESH,
        )

    def grad_copy(h, d):
        j, t = peer_level(d)
        n = level_rows[j]
        return pltpu.make_async_remote_copy(
            gsend.at[h, j - 2, :, pl.ds(t * n, n)],
            grecv.at[h, j - 2, :, pl.ds(t * n, n)],
            gr_s.at[h, d],
            gr_r.at[h, d],
            device_id={"seq": flip(me, QUAD * d)},
            device_id_type=pl.DeviceIdType.MESH,
        )

    barrier = pltpu.get_barrier_semaphore()
    for x in range(1, QUAD):
        pl.semaphore_signal(
            barrier, inc=1, device_id={"seq": flip(me, x)}, device_id_type=pl.DeviceIdType.MESH
        )
    for d in range(1, groups):
        pl.semaphore_signal(
            barrier,
            inc=1,
            device_id={"seq": flip(me, QUAD * d)},
            device_id_type=pl.DeviceIdType.MESH,
        )
    pl.semaphore_signal(
        barrier, inc=1, device_id={"head": 1 - core}, device_id_type=pl.DeviceIdType.MESH
    )
    pl.semaphore_wait(barrier, QUAD - 1 + groups - 1 + 1)

    for h in range(own_heads):
        for a in (1, 2, 0, 3):
            for x in (3, 1, 2, 0):
                in_copy(a, h, x).start()

    gain_loads = [
        pltpu.make_async_copy(src, gains.at[i], gain_s.at[i]) for i, src in enumerate((gain_q, gain_k))
    ]
    for load in gain_loads:
        load.start()
    for load in gain_loads:
        load.wait()
    gacc[...] = jnp.zeros_like(gacc)

    def wait_in(a, h):
        for x in range(1, QUAD):
            in_copy(a, h, x).wait_recv()
        in_copy(a, h, 0).wait()

    def norm_rows(raw):
        as_float = raw.astype(F32)
        inv = lax.rsqrt(jnp.mean(as_float * as_float, axis=-1, keepdims=True) + EPS)
        return as_float, inv

    chunks = total // rows

    def pyramid(read, write):
        def base(c, _):
            r = pl.ds(pl.multiple_of(c * rows, rows), rows)
            value = read(r)
            write(r, value)
            wide[r] = value.astype(F32)
            return 0

        lax.fori_loop(0, chunks, base, 0)
        for j in range(1, depth):
            n = level_rows[j]
            step = min(n, 256)
            for s in range(0, n, step):
                mean = 0.5 * (
                    wide[pl.ds(2 * s, step, stride=2)] + wide[pl.ds(2 * s + 1, step, stride=2)]
                )
                value = mean.astype(BF16)
                write(pl.ds(offs[j] + s, step), value)
                wide[pl.ds(s, step)] = value.astype(F32)

    def spread(ref, j, factor):
        n = level_rows[j]
        step = min(n, 256)
        for s in range(0, n, step):
            value = factor * ref[pl.ds(offs[j] + s, step)]
            for parity in range(2):
                dst = pl.ds(offs[j - 1] + 2 * s + parity, step, stride=2)
                ref[dst] = ref[dst] + value

    def gather_pairs(ref, j):
        n = level_rows[j]
        step = min(n, 256)
        for s in range(0, n, step):
            first = ref[pl.ds(offs[j - 1] + 2 * s, step, stride=2)]
            second = ref[pl.ds(offs[j - 1] + 2 * s + 1, step, stride=2)]
            ref[pl.ds(offs[j] + s, step)] = first + second

    def probs(q, k):
        return jnp.exp2(dot_nt(q, k) * exp_scale)

    def forward(weight, r, q, k, v):
        p = probs(q, k)
        pb = p.astype(BF16)
        num[r] = weight * dot_nn(pb, v)
        den[r] = weight * jnp.broadcast_to(jnp.sum(p, axis=-1, keepdims=True), (q.shape[0], DH))
        return pb

    def backward(weight, h, r, pb, q, k, v):
        sn = (weight * gnp[h, r]).astype(BF16)
        dv = dot_tn(pb, sn)
        dp = dot_nt(sn, v) + tiled(weight * gdp[h, r], k.shape[0])
        ds = (pb.astype(F32) * dp).astype(BF16)
        dq = inv_root * dot_nn(ds, k)
        dk = inv_root * dot_tn(ds, q)
        return dq, dk, dv

    gq = gains[0]
    gk = gains[1]

    def keys_and_values(h, _):
        def read_k(r):
            as_float, inv = norm_rows(rin[1, h, r])
            return (as_float * inv * gk).astype(BF16)

        def write_k(r, value):
            kvp[h, 0, r] = value

        def write_v(r, value):
            kvp[h, 1, r] = value

        wait_in(1, h)
        pyramid(read_k, write_k)
        wait_in(2, h)
        pyramid(lambda r: rin[2, h, r], write_v)
        for d in range(1, groups):
            kv_copy(h, d).start()
        return 0

    def forward_pass(h, _):
        def read_q(r):
            as_float, inv = norm_rows(rin[0, h, r])
            return (as_float * inv * gq).astype(BF16)

        def write_q(r, value):
            qp[h, r] = value

        wait_in(0, h)
        pyramid(read_q, write_q)

        def pair_forward(b, _):
            r = pl.ds(pl.multiple_of(b * rows, rows), rows)
            keys = pl.ds(pl.multiple_of(lax.div(b, 2) * 2 * rows, 2 * rows), 2 * rows)
            pair_p[h, r] = forward(1.0, r, qp[h, r], kvp[h, 0, keys], kvp[h, 1, keys])
            return 0

        lax.fori_loop(0, chunks, pair_forward, 0)

        def one_forward(b, _):
            r = pl.ds(pl.multiple_of(offs[1] + b * rows, rows), rows)
            keys = pl.ds(pl.multiple_of(offs[1] + (1 - b) * rows, rows), rows)
            one_p[h, b] = forward(2.0, r, qp[h, r], kvp[h, 0, keys], kvp[h, 1, keys])
            return 0

        lax.fori_loop(0, 2, one_forward, 0)
        for d in range(1, groups):
            kv_copy(h, d).wait_recv()
        for j in range(2, depth):
            r = pl.ds(offs[j], level_rows[j])
            up_p[j - 2, pl.ds(0, level_rows[j])] = forward(
                float(1 << j), r, qp[h, r], rkv[h, j - 2, 0], rkv[h, j - 2, 1]
            )
        for j in reversed(range(1, depth)):
            spread(num, j, 1.0)
            spread(den, j, 1.0)

        wait_in(3, h)

        def middle(c, _):
            r = pl.ds(pl.multiple_of(c * rows, rows), rows)
            inv = 1.0 / den[r]
            out_float = num[r] * inv
            oout[0, h, r] = out_float.astype(BF16)
            up = rin[3, h, r].astype(F32)
            gnp[h, r] = up * inv
            gdp[h, r] = -jnp.sum(up * out_float, axis=-1, keepdims=True) * inv
            return 0

        lax.fori_loop(0, chunks, middle, 0)
        for x in range(QUAD):
            out_copy(0, h, x).start()
        for j in range(1, depth):
            gather_pairs(gnp.at[h], j)
            gather_pairs(gdp.at[h], j)

        for j in range(2, depth):
            r = pl.ds(offs[j], level_rows[j])
            dq, dk, dv = backward(
                float(1 << j),
                h,
                r,
                up_p[j - 2, pl.ds(0, level_rows[j])],
                qp[h, r],
                rkv[h, j - 2, 0],
                rkv[h, j - 2, 1],
            )
            gqp[h, r] = dq
            gsend[h, j - 2, 0] = dk.astype(BF16)
            gsend[h, j - 2, 1] = dv.astype(BF16)
        for d in range(1, groups):
            grad_copy(h, d).start()
        return 0

    def backward_pass(h, _):
        def one_backward(b, _):
            r = pl.ds(pl.multiple_of(offs[1] + b * rows, rows), rows)
            keys = pl.ds(pl.multiple_of(offs[1] + (1 - b) * rows, rows), rows)
            dq, dk, dv = backward(
                2.0, h, r, one_p[h, b], qp[h, r], kvp[h, 0, keys], kvp[h, 1, keys]
            )
            gqp[h, r] = dq
            gkp[keys] = dk
            gvp[keys] = dv
            return 0

        lax.fori_loop(0, 2, one_backward, 0)

        def pair_backward(b, _):
            r = pl.ds(pl.multiple_of(b * 2 * rows, 2 * rows), 2 * rows)
            dq, dk, dv = backward(
                1.0, h, r, pair_p[h, r], qp[h, r], kvp[h, 0, r], kvp[h, 1, r]
            )
            gqp[h, r] = dq
            gkp[r] = dk
            gvp[r] = dv
            return 0

        lax.fori_loop(0, chunks // 2, pair_backward, 0)
        for j in reversed(range(1, depth)):
            spread(gqp.at[h], j, 0.5)

        def norm_back(a, src, gain, row):
            def step(c, acc):
                r = pl.ds(pl.multiple_of(c * rows, rows), rows)
                as_float, inv = norm_rows(rin[a, h, r])
                up = src[r]
                scaled = gain * up
                inner = jnp.mean(as_float * scaled, axis=-1, keepdims=True)
                normed = as_float * inv
                oout[1 + a, h, r] = (inv * (scaled - normed * (inv * inner))).astype(BF16)
                return acc + jnp.sum(normed * up, axis=0, keepdims=True)

            part = lax.fori_loop(0, chunks, step, jnp.zeros((1, DH), F32))
            gacc[row : row + 1] = gacc[row : row + 1] + part
            for x in range(QUAD):
                out_copy(1 + a, h, x).start()

        norm_back(0, gqp.at[h], gq, 0)

        for d in range(1, groups):
            grad_copy(h, d).wait_recv()
        for ref, which in ((gkp, 0), (gvp, 1)):
            for j in range(2, depth):
                n = level_rows[j]
                summed = grecv[h, j - 2, which, pl.ds(0, n)].astype(F32)
                for t in range(1, 1 << (j - 2)):
                    summed = summed + grecv[h, j - 2, which, pl.ds(t * n, n)].astype(F32)
                ref[pl.ds(offs[j], n)] = summed
            for j in reversed(range(1, depth)):
                spread(ref, j, 0.5)
            if which == 0:
                norm_back(1, gkp, gk, 1)

        def value_out(c, _):
            r = pl.ds(pl.multiple_of(c * rows, rows), rows)
            oout[3, h, r] = gvp[r].astype(BF16)
            return 0

        lax.fori_loop(0, chunks, value_out, 0)
        for x in range(QUAD):
            out_copy(3, h, x).start()
        return 0

    for h in range(own_heads):
        keys_and_values(h, 0)
        if h:
            backward_pass(h - 1, 0)
        forward_pass(h, 0)
    backward_pass(own_heads - 1, 0)

    def gain_exchange(landing, sends, recvs, peers):
        copies = [
            pltpu.make_async_remote_copy(
                gacc,
                landing.at[i],
                sends.at[i],
                recvs.at[i],
                device_id=peer,
                device_id_type=pl.DeviceIdType.MESH,
            )
            for i, peer in enumerate(peers)
        ]
        for copy in copies:
            copy.start()
        for copy in copies:
            copy.wait()
        summed = gacc[...]
        for i in range(len(peers)):
            summed = summed + landing[i]
        gacc[...] = summed

    gain_exchange(gc, gc_s, gc_r, [{"head": 1 - core}])
    if groups > 1:
        gain_exchange(gb, gb_s, gb_r, [{"seq": flip(me, QUAD * d)} for d in range(1, groups)])
    gain_exchange(ga, ga_s, ga_r, [{"seq": flip(me, x)} for x in range(1, QUAD)])
    gain_out[...] = gacc[0:2] * (1.0 / math.sqrt(rows * seq_count * HEADS))

    def finish(h, _):
        for a in range(4):
            for x in range(1, QUAD):
                in_copy(a, h, x).wait_send()
                out_copy(a, h, x).wait_send()
                out_copy(a, h, x).wait_recv()
            out_copy(a, h, 0).wait()
        for d in range(1, groups):
            kv_copy(h, d).wait_send()
            grad_copy(h, d).wait_send()
        return 0

    lax.fori_loop(0, own_heads, finish, 0)


def store_kernel(a0, a1, a2, a3, gains, o0, o1, o2, o3, gains_out, sems):
    copies = [
        pltpu.make_async_copy(src, dst, sems.at[i])
        for i, (src, dst) in enumerate(((a0, o0), (a1, o1), (a2, o2), (a3, o3)))
    ]
    for copy in copies:
        copy.start()
    gains_out[...] = gains[...]
    for copy in copies:
        copy.wait()


def per_device(queries, key_vectors, value_vectors, gain_query, gain_key, grad_out):
    rows, width = queries.shape
    seq_count = lax.axis_size("seq")
    own_heads = width // DH // QUAD
    depth = seq_count.bit_length() - 1
    groups = seq_count // QUAD
    total = QUAD * rows
    ups = max(depth - 2, 1)
    dma = pltpu.SemaphoreType.DMA
    any_spec = pl.BlockSpec(memory_space=pl.ANY)
    hbm_spec = pl.BlockSpec(memory_space=pltpu.HBM)
    vmem_spec = pl.BlockSpec(memory_space=pltpu.VMEM)
    like = jax.ShapeDtypeStruct((rows, width), BF16)
    out = pl.pallas_call(
        functools.partial(kernel, seq_count, rows, own_heads),
        out_shape=(like, like, like, like, jax.ShapeDtypeStruct((2, DH), F32)),
        in_specs=[hbm_spec] * 6,
        out_specs=(any_spec,) * 4 + (vmem_spec,),
        scratch_shapes=[
            pltpu.VMEM((4, own_heads, total, DH), BF16),
            pltpu.VMEM((4, own_heads, total, DH), BF16),
            pltpu.VMEM((own_heads, 2 * total, DH), BF16),
            pltpu.VMEM((own_heads, 2, 2 * total, DH), BF16),
            pltpu.VMEM((own_heads, ups, 2, rows, DH), BF16),
            pltpu.VMEM((own_heads, ups, 2, rows, DH), BF16),
            pltpu.VMEM((own_heads, ups, 2, rows, DH), BF16),
            pltpu.VMEM((total, DH), F32),
            pltpu.VMEM((2 * total, DH), F32),
            pltpu.VMEM((2 * total, DH), F32),
            pltpu.VMEM((own_heads, 2 * total, DH), F32),
            pltpu.VMEM((own_heads, 2 * total, DH), F32),
            pltpu.VMEM((own_heads, 2 * total, DH), F32),
            pltpu.VMEM((2 * total, DH), F32),
            pltpu.VMEM((2 * total, DH), F32),
            pltpu.VMEM((own_heads, total, 2 * rows), BF16),
            pltpu.VMEM((own_heads, 2, rows, rows), BF16),
            pltpu.VMEM((ups, rows, rows), BF16),
            pltpu.VMEM((2, 1, DH), F32),
            pltpu.VMEM((8, DH), F32),
            pltpu.VMEM((QUAD, 8, DH), F32),
            pltpu.VMEM((groups, 8, DH), F32),
            pltpu.VMEM((1, 8, DH), F32),
        ]
        + [dma((4, own_heads, QUAD))] * 4
        + [dma((own_heads, groups))] * 4
        + [dma((QUAD,))] * 2
        + [dma((groups,))] * 2
        + [dma((1,))] * 2
        + [dma((2,))],
        compiler_params=pltpu.CompilerParams(
            collective_id=0, has_side_effects=True, vmem_limit_bytes=48 << 20
        ),
    )(
        *(
            pltpu.with_memory_space_constraint(x, pltpu.HBM)
            for x in (
                queries, key_vectors, value_vectors, grad_out,
                gain_query.reshape(1, DH), gain_key.reshape(1, DH),
            )
        )
    )
    return pl.pallas_call(
        store_kernel,
        out_shape=(like, like, like, like, jax.ShapeDtypeStruct((2, DH), F32)),
        in_specs=[any_spec] * 4 + [vmem_spec],
        out_specs=(hbm_spec,) * 4 + (vmem_spec,),
        scratch_shapes=[dma((4,))],
        compiler_params=pltpu.CompilerParams(vmem_limit_bytes=4 << 20),
    )(*out)


def solution(mesh):
    in_specs = (P("seq", "head"), P("seq", "head"), P("seq", "head"), P(), P(), P("seq", "head"))
    out_specs = (P("seq", "head"), P("seq", "head"), P("seq", "head"), P("seq", "head"), P())
    return jax.shard_map(
        per_device, mesh=mesh, in_specs=in_specs, out_specs=out_specs, check_vma=False
    )
```

profile of v0, /device:TPU:0, one launch (start us, length us, event | category | flops | bytes accessed | tf_op | source)
XLA Modules:
  0.0 57.6 jit_solution(17859560715819205633)
XLA Ops:
  0.6 55.1 %shard_map.101 = (bf16[256,1024]{1,0:T(8,128)(2,1)S(1)}, bf16[256,1024]{1,0:T(8,128)(2,1)S(1)}, bf16[256,1024]{1,0:T(8,128)(2,1)S(1)}, bf16[256,1024]{1,0:T(8,128)(2,1)S(1)}, f32[2,128]{1,0:T(2,128)S(1)}) custom-call(bf16[256,1024]{1,0:T(8,128)(2,1)} %q_hbm.1, bf16[256,1024]{1,0:T(8,128)(2,1)} %k_hbm.1, bf16[256,1024]{1,0:T(8,128)(2,1)} %v_hbm.1, ...), custom_call_target="tpu_custom_call" | custom-call | tf_op jit(solution)/shard_map/pallas_call | solution.py:468
  55.7 1.9 %shard_map.102 = (bf16[256,1024]{1,0:T(8,128)(2,1)}, bf16[256,1024]{1,0:T(8,128)(2,1)}, bf16[256,1024]{1,0:T(8,128)(2,1)}, bf16[256,1024]{1,0:T(8,128)(2,1)}, f32[2,128]{1,0:T(2,128)}) custom-call(bf16[256,1024]{1,0:T(8,128)(2,1)S(1)} %get-tuple-element.10.a0, bf16[256,1024]{1,0:T(8,128)(2,1)S(1)} %get-tuple-element.11.a1, ...), custom_call_target="tpu_custom_call" | custom-call | tf_op jit(solution)/shard_map/pallas_call | solution.py:516
where the time goes:
time: 57.8 us; the launch traced here: 57.6 us
  Pallas kernels  57 us (99%)
  between operations  0.64 us (1%)
    pallas_call x1, Pallas kernels, per_device(): pl.pallas_call(functools.partial(kernel, seq_count, rows, own_heads), out...  55.1 us
    pallas_call x1, Pallas kernels, per_device(): pl.pallas_call(store_kernel, out_shape=(like, like, like, like, jax.Shape...  1.91 us

commit v1 on v0

--- a/solution.py
+++ b/solution.py
@@ -39,6 +39,11 @@
     return lax.dot_general(a, b, (((0,), (0,)), ((), ())), preferred_element_type=F32)
 
 
+def unrolled(count, step):
+    for i in range(count):
+        step(i, 0)
+
+
 def tiled(lanes, width):
     return jnp.concatenate([lanes] * (width // lanes.shape[1]), axis=1)
 
@@ -48,8 +53,8 @@
     q_hbm, k_hbm, v_hbm, g_hbm, gain_q, gain_k,
     att_hbm, dq_hbm, dk_hbm, dv_hbm, gain_out,
     rin, oout, qp, kvp, rkv, gsend, grecv, wide, num, den, gnp, gdp, gqp, gkp, gvp,
-    pair_p, one_p, up_p, gains, gacc, ga, gb, gc,
-    in_s, in_r, out_s, out_r, kv_s, kv_r, gr_s, gr_r, ga_s, ga_r, gb_s, gb_r, gc_s, gc_r, gain_s,
+    pair_p, one_p, up_p, gains, gacc, gsum, ga, gb, gc, rms,
+    in_s, in_r, out_s, out_r, kv_s, kv_r, gr_s, gr_r, ga_s, ga_r, gb_s, gb_r, gc_s, gc_r, gain_s, ready,
 ):
     depth = seq_count.bit_length() - 1
     groups = seq_count // QUAD
@@ -61,6 +66,7 @@
     me = lax.axis_index("seq")
     core = lax.axis_index("head")
     member = lax.rem(me, QUAD)
+    group = lax.div(me, QUAD)
     inputs = (q_hbm, k_hbm, v_hbm, g_hbm)
     outputs = (att_hbm, dq_hbm, dk_hbm, dv_hbm)
 
@@ -131,17 +137,25 @@
         pl.semaphore_signal(
             barrier, inc=1, device_id={"seq": flip(me, x)}, device_id_type=pl.DeviceIdType.MESH
         )
-    for d in range(1, groups):
-        pl.semaphore_signal(
-            barrier,
-            inc=1,
-            device_id={"seq": flip(me, QUAD * d)},
-            device_id_type=pl.DeviceIdType.MESH,
-        )
     pl.semaphore_signal(
         barrier, inc=1, device_id={"head": 1 - core}, device_id_type=pl.DeviceIdType.MESH
     )
-    pl.semaphore_wait(barrier, QUAD - 1 + groups - 1 + 1)
+    pl.semaphore_wait(barrier, QUAD + group)
+
+    def greet(semaphore):
+        def step(other, _):
+            pl.semaphore_signal(
+                semaphore,
+                inc=1,
+                device_id={"seq": other * QUAD + member},
+                device_id_type=pl.DeviceIdType.MESH,
+            )
+            return 0
+
+        return step
+
+    lax.fori_loop(group + 1, groups, greet(barrier), 0)
+    lax.fori_loop(0, group, greet(ready), 0)
 
     for h in range(own_heads):
         for a in (1, 2, 0, 3):
@@ -171,13 +185,12 @@
 
     def pyramid(read, write):
         def base(c, _):
-            r = pl.ds(pl.multiple_of(c * rows, rows), rows)
+            r = pl.ds(c * rows, rows)
             value = read(r)
             write(r, value)
             wide[r] = value.astype(F32)
-            return 0
-
-        lax.fori_loop(0, chunks, base, 0)
+
+        unrolled(chunks, base)
         for j in range(1, depth):
             n = level_rows[j]
             step = min(n, 256)
@@ -212,8 +225,9 @@
     def forward(weight, r, q, k, v):
         p = probs(q, k)
         pb = p.astype(BF16)
-        num[r] = weight * dot_nn(pb, v)
-        den[r] = weight * jnp.broadcast_to(jnp.sum(p, axis=-1, keepdims=True), (q.shape[0], DH))
+        both = dot_nn(pb, jnp.concatenate([v, jnp.ones_like(v)], axis=1))
+        num[r] = weight * both[:, :DH]
+        den[r] = weight * both[:, DH:]
         return pb
 
     def backward(weight, h, r, pb, q, k, v):
@@ -225,12 +239,32 @@
         dk = inv_root * dot_tn(ds, q)
         return dq, dk, dv
 
+    def gain_copies(src, landing, sends, recvs, peers):
+        return [
+            pltpu.make_async_remote_copy(
+                src,
+                landing.at[i],
+                sends.at[i],
+                recvs.at[i],
+                device_id=peer,
+                device_id_type=pl.DeviceIdType.MESH,
+            )
+            for i, peer in enumerate(peers)
+        ]
+
+    quad_gains = gain_copies(gacc, ga, ga_s, ga_r, [{"seq": flip(me, x)} for x in range(1, QUAD)])
+    group_gains = gain_copies(
+        gsum.at[0], gb, gb_s, gb_r, [{"seq": flip(me, QUAD * d)} for d in range(1, groups)]
+    )
+    core_gains = gain_copies(gsum.at[1], gc, gc_s, gc_r, [{"head": 1 - core}])
+
     gq = gains[0]
     gk = gains[1]
 
     def keys_and_values(h, _):
         def read_k(r):
             as_float, inv = norm_rows(rin[1, h, r])
+            rms[1, h, r] = jnp.broadcast_to(inv, as_float.shape)
             return (as_float * inv * gk).astype(BF16)
 
         def write_k(r, value):
@@ -243,6 +277,12 @@
         pyramid(read_k, write_k)
         wait_in(2, h)
         pyramid(lambda r: rin[2, h, r], write_v)
+        if h == 0:
+
+            @pl.when(group < groups - 1)
+            def _():
+                pl.semaphore_wait(ready, groups - 1 - group)
+
         for d in range(1, groups):
             kv_copy(h, d).start()
         return 0
@@ -250,6 +290,7 @@
     def forward_pass(h, _):
         def read_q(r):
             as_float, inv = norm_rows(rin[0, h, r])
+            rms[0, h, r] = jnp.broadcast_to(inv, as_float.shape)
             return (as_float * inv * gq).astype(BF16)
 
         def write_q(r, value):
@@ -259,20 +300,17 @@
         pyramid(read_q, write_q)
 
         def pair_forward(b, _):
-            r = pl.ds(pl.multiple_of(b * rows, rows), rows)
-            keys = pl.ds(pl.multiple_of(lax.div(b, 2) * 2 * rows, 2 * rows), 2 * rows)
-            pair_p[h, r] = forward(1.0, r, qp[h, r], kvp[h, 0, keys], kvp[h, 1, keys])
-            return 0
-
-        lax.fori_loop(0, chunks, pair_forward, 0)
+            r = pl.ds(b * 2 * rows, 2 * rows)
+            pair_p[h, r] = forward(1.0, r, qp[h, r], kvp[h, 0, r], kvp[h, 1, r])
+
+        unrolled(chunks // 2, pair_forward)
 
         def one_forward(b, _):
-            r = pl.ds(pl.multiple_of(offs[1] + b * rows, rows), rows)
-            keys = pl.ds(pl.multiple_of(offs[1] + (1 - b) * rows, rows), rows)
+            r = pl.ds(offs[1] + b * rows, rows)
+            keys = pl.ds(offs[1] + (1 - b) * rows, rows)
             one_p[h, b] = forward(2.0, r, qp[h, r], kvp[h, 0, keys], kvp[h, 1, keys])
-            return 0
-
-        lax.fori_loop(0, 2, one_forward, 0)
+
+        unrolled(2, one_forward)
         for d in range(1, groups):
             kv_copy(h, d).wait_recv()
         for j in range(2, depth):
@@ -321,52 +359,61 @@
             grad_copy(h, d).start()
         return 0
 
-    def backward_pass(h, _):
+    def norm_back(a, h, src, gain, row):
+        some = min(rows, 128)
+
+        def step(c, acc):
+            r = pl.ds(pl.multiple_of(c * some, some), some)
+            inv = rms[a, h, r]
+            normed = rin[a, h, r].astype(F32) * inv
+            scaled = gain * src[r]
+            both = normed * scaled
+            inner = jnp.mean(both, axis=-1, keepdims=True)
+            oout[1 + a, h, r] = (inv * (scaled - normed * inner)).astype(BF16)
+            return acc + jnp.sum(both.reshape(some // 8, 8, DH), axis=0)
+
+        part = lax.fori_loop(0, total // some, step, jnp.zeros((8, DH), F32), unroll=2)
+        part = jnp.sum(part, axis=0, keepdims=True) / gain
+        gacc[row : row + 1] = gacc[row : row + 1] + part
+        if h == own_heads - 1 and row == 1:
+            for copy in quad_gains:
+                copy.start()
+            for held in (1,):
+                for x in range(QUAD):
+                    out_copy(held, h, x).start()
+        if h < own_heads - 1 or row == 1:
+            for x in range(QUAD):
+                out_copy(1 + a, h, x).start()
+
+    def backward_queries(h):
         def one_backward(b, _):
-            r = pl.ds(pl.multiple_of(offs[1] + b * rows, rows), rows)
-            keys = pl.ds(pl.multiple_of(offs[1] + (1 - b) * rows, rows), rows)
+            r = pl.ds(offs[1] + b * rows, rows)
+            keys = pl.ds(offs[1] + (1 - b) * rows, rows)
             dq, dk, dv = backward(
                 2.0, h, r, one_p[h, b], qp[h, r], kvp[h, 0, keys], kvp[h, 1, keys]
             )
             gqp[h, r] = dq
             gkp[keys] = dk
             gvp[keys] = dv
-            return 0
-
-        lax.fori_loop(0, 2, one_backward, 0)
+
+        unrolled(2, one_backward)
 
         def pair_backward(b, _):
-            r = pl.ds(pl.multiple_of(b * 2 * rows, 2 * rows), 2 * rows)
+            r = pl.ds(b * 2 * rows, 2 * rows)
             dq, dk, dv = backward(
                 1.0, h, r, pair_p[h, r], qp[h, r], kvp[h, 0, r], kvp[h, 1, r]
             )
             gqp[h, r] = dq
             gkp[r] = dk
             gvp[r] = dv
-            return 0
-
-        lax.fori_loop(0, chunks // 2, pair_backward, 0)
+
+        unrolled(chunks // 2, pair_backward)
         for j in reversed(range(1, depth)):
             spread(gqp.at[h], j, 0.5)
 
-        def norm_back(a, src, gain, row):
-            def step(c, acc):
-                r = pl.ds(pl.multiple_of(c * rows, rows), rows)
-                as_float, inv = norm_rows(rin[a, h, r])
-                up = src[r]
-                scaled = gain * up
-                inner = jnp.mean(as_float * scaled, axis=-1, keepdims=True)
-                normed = as_float * inv
-                oout[1 + a, h, r] = (inv * (scaled - normed * (inv * inner))).astype(BF16)
-                return acc + jnp.sum(normed * up, axis=0, keepdims=True)
-
-            part = lax.fori_loop(0, chunks, step, jnp.zeros((1, DH), F32))
-            gacc[row : row + 1] = gacc[row : row + 1] + part
-            for x in range(QUAD):
-                out_copy(1 + a, h, x).start()
-
-        norm_back(0, gqp.at[h], gq, 0)
-
+        norm_back(0, h, gqp.at[h], gq, 0)
+
+    def backward_keys(h):
         for d in range(1, groups):
             grad_copy(h, d).wait_recv()
         for ref, which in ((gkp, 0), (gvp, 1)):
@@ -379,7 +426,7 @@
             for j in reversed(range(1, depth)):
                 spread(ref, j, 0.5)
             if which == 0:
-                norm_back(1, gkp, gk, 1)
+                norm_back(1, h, gkp, gk, 1)
 
         def value_out(c, _):
             r = pl.ds(pl.multiple_of(c * rows, rows), rows)
@@ -389,41 +436,28 @@
         lax.fori_loop(0, chunks, value_out, 0)
         for x in range(QUAD):
             out_copy(3, h, x).start()
-        return 0
 
     for h in range(own_heads):
         keys_and_values(h, 0)
         if h:
-            backward_pass(h - 1, 0)
+            backward_queries(h - 1)
         forward_pass(h, 0)
-    backward_pass(own_heads - 1, 0)
-
-    def gain_exchange(landing, sends, recvs, peers):
-        copies = [
-            pltpu.make_async_remote_copy(
-                gacc,
-                landing.at[i],
-                sends.at[i],
-                recvs.at[i],
-                device_id=peer,
-                device_id_type=pl.DeviceIdType.MESH,
-            )
-            for i, peer in enumerate(peers)
-        ]
-        for copy in copies:
-            copy.start()
+        if h:
+            backward_keys(h - 1)
+    backward_queries(own_heads - 1)
+    backward_keys(own_heads - 1)
+
+    total_gain = gacc[...]
+    for round, (copies, landing) in enumerate(((quad_gains, ga), (group_gains, gb), (core_gains, gc))):
+        if round:
+            gsum[round - 1] = total_gain
+            for copy in copies:
+                copy.start()
         for copy in copies:
             copy.wait()
-        summed = gacc[...]
-        for i in range(len(peers)):
-            summed = summed + landing[i]
-        gacc[...] = summed
-
-    gain_exchange(gc, gc_s, gc_r, [{"head": 1 - core}])
-    if groups > 1:
-        gain_exchange(gb, gb_s, gb_r, [{"seq": flip(me, QUAD * d)} for d in range(1, groups)])
-    gain_exchange(ga, ga_s, ga_r, [{"seq": flip(me, x)} for x in range(1, QUAD)])
-    gain_out[...] = gacc[0:2] * (1.0 / math.sqrt(rows * seq_count * HEADS))
+        for i in range(len(copies)):
+            total_gain = total_gain + landing[i]
+    gain_out[...] = total_gain[0:2] * (1.0 / math.sqrt(rows * seq_count * HEADS))
 
     def finish(h, _):
         for a in range(4):
@@ -491,16 +525,18 @@
             pltpu.VMEM((ups, rows, rows), BF16),
             pltpu.VMEM((2, 1, DH), F32),
             pltpu.VMEM((8, DH), F32),
+            pltpu.VMEM((2, 8, DH), F32),
             pltpu.VMEM((QUAD, 8, DH), F32),
             pltpu.VMEM((groups, 8, DH), F32),
             pltpu.VMEM((1, 8, DH), F32),
+            pltpu.VMEM((2, own_heads, total, DH), F32),
         ]
         + [dma((4, own_heads, QUAD))] * 4
         + [dma((own_heads, groups))] * 4
         + [dma((QUAD,))] * 2
         + [dma((groups,))] * 2
         + [dma((1,))] * 2
-        + [dma((2,))],
+        + [dma((2,)), pltpu.SemaphoreType.REGULAR],
         compiler_params=pltpu.CompilerParams(
             collective_id=0, has_side_effects=True, vmem_limit_bytes=48 << 20
         ),

time: 57.8 us -> 56.2 us (0.972)
  Pallas kernels: 57 us -> 55.4 us
    pallas_call x1, Pallas kernels: 55.1 us -> 53.5 us  [per_device(): pl.pallas_call(functools.partial(kernel, seq_count, rows, own_heads), out...]
where the time goes in v1:
time: 56.2 us; the launch traced here: 56 us
  Pallas kernels  55.4 us (99%)
  between operations  0.64 us (1%)
    pallas_call x1, Pallas kernels, per_device(): pl.pallas_call(functools.partial(kernel, seq_count, rows, own_heads), out...  53.5 us
    pallas_call x1, Pallas kernels, per_device(): pl.pallas_call(store_kernel, out_shape=(like, like, like, like, jax.Shape...  1.91 us

profile of v1, /device:TPU:0, one launch (start us, length us, event | category | flops | bytes accessed | tf_op | source)
XLA Modules:
  0.0 56.0 jit_solution(4525246718370975487)
XLA Ops:
  0.6 53.5 %shard_map.101 = (bf16[256,1024]{1,0:T(8,128)(2,1)S(1)}, bf16[256,1024]{1,0:T(8,128)(2,1)S(1)}, bf16[256,1024]{1,0:T(8,128)(2,1)S(1)}, bf16[256,1024]{1,0:T(8,128)(2,1)S(1)}, f32[2,128]{1,0:T(2,128)S(1)}) custom-call(bf16[256,1024]{1,0:T(8,128)(2,1)} %q_hbm.1, bf16[256,1024]{1,0:T(8,128)(2,1)} %k_hbm.1, bf16[256,1024]{1,0:T(8,128)(2,1)} %v_hbm.1, ...), custom_call_target="tpu_custom_call" | custom-call | tf_op jit(solution)/shard_map/pallas_call | solution.py:502
  54.1 1.9 %shard_map.102 = (bf16[256,1024]{1,0:T(8,128)(2,1)}, bf16[256,1024]{1,0:T(8,128)(2,1)}, bf16[256,1024]{1,0:T(8,128)(2,1)}, bf16[256,1024]{1,0:T(8,128)(2,1)}, f32[2,128]{1,0:T(2,128)}) custom-call(bf16[256,1024]{1,0:T(8,128)(2,1)S(1)} %get-tuple-element.10.a0, bf16[256,1024]{1,0:T(8,128)(2,1)S(1)} %get-tuple-element.11.a1, ...), custom_call_target="tpu_custom_call" | custom-call | tf_op jit(solution)/shard_map/pallas_call | solution.py:552

commit v2 on v1

--- a/solution.py
+++ b/solution.py
@@ -157,10 +157,11 @@
     lax.fori_loop(group + 1, groups, greet(barrier), 0)
     lax.fori_loop(0, group, greet(ready), 0)
 
-    for h in range(own_heads):
-        for a in (1, 2, 0, 3):
-            for x in (3, 1, 2, 0):
-                in_copy(a, h, x).start()
+    for pair in ((1, 2), (0, 3)):
+        for h in range(own_heads):
+            for a in pair:
+                for x in (3, 1, 2, 0):
+                    in_copy(a, h, x).start()
 
     gain_loads = [
         pltpu.make_async_copy(src, gains.at[i], gain_s.at[i]) for i, src in enumerate((gain_q, gain_k))
@@ -283,7 +284,7 @@
             def _():
                 pl.semaphore_wait(ready, groups - 1 - group)
 
-        for d in range(1, groups):
+        for d in reversed(range(1, groups)):
             kv_copy(h, d).start()
         return 0
 
@@ -335,8 +336,9 @@
             return 0
 
         lax.fori_loop(0, chunks, middle, 0)
-        for x in range(QUAD):
-            out_copy(0, h, x).start()
+        if h < own_heads - 1:
+            for x in range(QUAD):
+                out_copy(0, h, x).start()
         for j in range(1, depth):
             gather_pairs(gnp.at[h], j)
             gather_pairs(gdp.at[h], j)
@@ -355,7 +357,7 @@
             gqp[h, r] = dq
             gsend[h, j - 2, 0] = dk.astype(BF16)
             gsend[h, j - 2, 1] = dv.astype(BF16)
-        for d in range(1, groups):
+        for d in reversed(range(1, groups)):
             grad_copy(h, d).start()
         return 0
 
@@ -378,7 +380,7 @@
         if h == own_heads - 1 and row == 1:
             for copy in quad_gains:
                 copy.start()
-            for held in (1,):
+            for held in (0, 1):
                 for x in range(QUAD):
                     out_copy(held, h, x).start()
         if h < own_heads - 1 or row == 1:
@@ -439,6 +441,7 @@
 
     for h in range(own_heads):
         keys_and_values(h, 0)
+    for h in range(own_heads):
         if h:
             backward_queries(h - 1)
         forward_pass(h, 0)

time: 56.2 us -> 55.1 us (0.980)
  Pallas kernels: 55.4 us -> 54.3 us
    pallas_call x1, Pallas kernels: 53.5 us -> 52.4 us  [per_device(): pl.pallas_call(functools.partial(kernel, seq_count, rows, own_heads), out...]
where the time goes in v2:
time: 55.1 us; the launch traced here: 54.9 us
  Pallas kernels  54.3 us (99%)
  between operations  0.64 us (1%)
    pallas_call x1, Pallas kernels, per_device(): pl.pallas_call(functools.partial(kernel, seq_count, rows, own_heads), out...  52.4 us
    pallas_call x1, Pallas kernels, per_device(): pl.pallas_call(store_kernel, out_shape=(like, like, like, like, jax.Shape...  1.91 us

profile of v2, /device:TPU:0, one launch (start us, length us, event | category | flops | bytes accessed | tf_op | source)
XLA Modules:
  0.0 54.9 jit_solution(6373275976617322948)
XLA Ops:
  0.6 52.4 %shard_map.101 = (bf16[256,1024]{1,0:T(8,128)(2,1)S(1)}, bf16[256,1024]{1,0:T(8,128)(2,1)S(1)}, bf16[256,1024]{1,0:T(8,128)(2,1)S(1)}, bf16[256,1024]{1,0:T(8,128)(2,1)S(1)}, f32[2,128]{1,0:T(2,128)S(1)}) custom-call(bf16[256,1024]{1,0:T(8,128)(2,1)} %q_hbm.1, bf16[256,1024]{1,0:T(8,128)(2,1)} %k_hbm.1, bf16[256,1024]{1,0:T(8,128)(2,1)} %v_hbm.1, ...), custom_call_target="tpu_custom_call" | custom-call | tf_op jit(solution)/shard_map/pallas_call | solution.py:505
  53.0 1.9 %shard_map.102 = (bf16[256,1024]{1,0:T(8,128)(2,1)}, bf16[256,1024]{1,0:T(8,128)(2,1)}, bf16[256,1024]{1,0:T(8,128)(2,1)}, bf16[256,1024]{1,0:T(8,128)(2,1)}, f32[2,128]{1,0:T(2,128)}) custom-call(bf16[256,1024]{1,0:T(8,128)(2,1)S(1)} %get-tuple-element.10.a0, bf16[256,1024]{1,0:T(8,128)(2,1)S(1)} %get-tuple-element.11.a1, ...), custom_call_target="tpu_custom_call" | custom-call | tf_op jit(solution)/shard_map/pallas_call | solution.py:555
